TPU v7x, 512 devices: a whole 4x4x16 slice. The times are simulated.
512 devices in a mesh: gx: 16 (over z), gy: 4 (over x), gz: 8 (over y, core).
Axes of the slice: x: 4, y: 4, z: 16, core: 2. Of those that a mesh axis runs over, the one named last changes fastest.
Arguments:
- flow: float32 [4, 128, 64, 1024], P(None, 'gx', 'gy', 'gz'), may hold values from -3 to 3
- basis: float32 [127, 3, 131072], P(None, None, ('gx', 'gy', 'gz')), may hold values from -1150 to 1150
- sample: int32 [131072], P(('gx', 'gy', 'gz')), may hold values from 0 to 16383
Outputs:
- flow_next: float32 [4, 128, 64, 1024], P(None, 'gx', 'gy', 'gz')
- basis_next: float32 [128, 3, 131072], P(None, None, ('gx', 'gy', 'gz'))
- factor: float32 [128, 128], replicated
All inputs are finite; a program needn't handle non-finite values.
Results may differ from a plain program's by a relative error of at most 0.000065.
Values sent between devices are 32-bit elements; how exact they have to be, the bound alone decides.
A program may use at most 64 MiB of HBM per device.

v0:
```python
import jax
import jax.numpy as jnp
from jax import lax
from jax.sharding import PartitionSpec as P

DT_STEP = 0.35
VISCOSITY = 0.2
SOUND_SQ = 1.0
DRIVING = 0.5


def padded(block, sides, width, periodic):
    for axis, dim in sides:
        count = lax.axis_size(axis)
        forward = [(i, i + 1) for i in range(count - 1)]
        if periodic:
            forward.append((count - 1, 0))
        backward = [(target, source) for source, target in forward]
        low = lax.ppermute(
            lax.slice_in_dim(block, block.shape[dim] - width, None, axis=dim), axis, forward
        )
        high = lax.ppermute(lax.slice_in_dim(block, 0, width, axis=dim), axis, backward)
        block = jnp.concatenate([low, block, high], axis=dim)
    return block


def rates(ext):
    centre = ext[:, 1:-1, 1:-1, 1:-1]
    x_plus = ext[:, 2:, 1:-1, 1:-1]
    x_minus = ext[:, :-2, 1:-1, 1:-1]
    y_plus = ext[:, 1:-1, 2:, 1:-1]
    y_minus = ext[:, 1:-1, :-2, 1:-1]
    z_plus = ext[:, 1:-1, 1:-1, 2:]
    z_minus = ext[:, 1:-1, 1:-1, :-2]
    slope_x = 0.5 * (x_plus - x_minus)
    slope_y = 0.5 * (y_plus - y_minus)
    slope_z = 0.5 * (z_plus - z_minus)
    laplace = x_plus + x_minus + (y_plus + y_minus) + (z_plus + z_minus) - 6.0 * centre
    advect = centre[0] * slope_x[:3] + centre[1] * slope_y[:3] + centre[2] * slope_z[:3]
    pressure = jnp.stack([slope_x[3], slope_y[3], slope_z[3]])
    forcing = jnp.array([DRIVING, 0.0, 0.0], dtype=jnp.float32).reshape(3, 1, 1, 1)
    velocity = VISCOSITY * laplace[:3] - advect - pressure + forcing
    density = -SOUND_SQ * (slope_x[0] + slope_y[1] + slope_z[2])
    return jnp.concatenate([velocity, density[None]], axis=0)


def extend_one(fields):
    walled = padded(fields, (("gy", 2),), 1, False)
    return padded(walled, (("gx", 1), ("gz", 3)), 1, True)


def local(flow, basis, sample):
    points = basis.shape[2]
    modes = basis.shape[0]
    count = 3.0 * points * lax.axis_size("gx") * lax.axis_size("gy") * lax.axis_size("gz")
    section_one = flow + DT_STEP * rates(extend_one(flow))
    section_two = 0.75 * flow + 0.25 * (section_one + DT_STEP * rates(extend_one(section_one)))
    flow_next = 1.0 / 3.0 * flow + 2.0 / 3.0 * (
        section_two + DT_STEP * rates(extend_one(section_two))
    )
    velocity = flow_next[:3].reshape(3, -1)
    snapshot = jnp.take(velocity, sample, axis=1)
    stacked = jnp.concatenate([basis, snapshot[None]], axis=0).reshape(modes + 1, 3 * points)
    local_gram = jnp.dot(
        stacked, stacked.T, precision=lax.Precision.HIGHEST, preferred_element_type=jnp.float32
    )
    gram = lax.psum(local_gram, ("gx", "gy", "gz")) / count
    lower = jnp.linalg.cholesky(gram)
    basis_next = jax.scipy.linalg.solve_triangular(lower, stacked, lower=True).reshape(
        modes + 1, 3, points
    )
    return (flow_next, basis_next, lower.T)


def solution(mesh):
    return jax.shard_map(
        local,
        mesh=mesh,
        in_specs=(
            P(None, "gx", "gy", "gz"),
            P(None, None, ("gx", "gy", "gz")),
            P(("gx", "gy", "gz")),
        ),
        out_specs=(P(None, "gx", "gy", "gz"), P(None, None, ("gx", "gy", "gz")), P()),
        check_vma=False,
    )
```

profile of v0, /device:TPU:1, one launch (start us, length us, event | category | flops | bytes accessed | tf_op | source)
XLA Modules:
  0.0 582.4 jit_solution(7620865436270588193)
XLA Ops:
  8.3 3.9 collective-permute-start
  12.2 1.3 collective-permute-start.1
  14.4 2.2 collective-permute-done.1
  17.5 11.1 %collective-permute-start.2 = (f32[4,1,18,128]{3,2,1,0:T(8,128)S(1)}, f32[4,1,18,128]{3,2,1,0:T(8,128)S(1)}, u32[]{:S(2)}, u32[]{:S(2)}) collective-permute-start(f32[4,1,18,128]{3,2,1,0:T(8,128)S(1)} %get-tuple-element.41), channel_id=1, source_target_pairs={{32,0},{64,32},{96,64},{128,96},{160,128},{192,160},{224,192},{256... | collective-permute-start | bytes 110600 | tf_op jit(solution)/shard_map/ppermute | solution.py:22
  28.6 1.9 collective-permute-start.3
  31.2 3.4 collective-permute-done.3
  35.9 3.5 collective-permute-start.4
  40.6 1.6 subtract_multiply_fusion.5
  42.2 5.2 collective-permute-done.4
  47.4 1.4 subtract_multiply_fusion.4
  48.9 1.5 fusion.24
  50.4 3.1 collective-permute-start.6
  53.6 1.3 collective-permute-start.7
  54.9 3.1 collective-permute-done.7
  58.1 1.9 collective-permute-start.8
  60.0 3.4 collective-permute-start.9
  63.4 2.6 collective-permute-done.9
  66.3 4.2 collective-permute-start.10
  70.7 6.5 %collective-permute-done.10 = f32[4,10,18,1]{3,2,1,0:T(8,128)S(1)} collective-permute-done((f32[4,10,18,1]{3,2,1,0:T(8,128)S(1)}, f32[4,10,18,1]{3,2,1,0:T(8,128)S(1)}, u32[]{:S(2)}, u32[]{:S(2)}) %collective-permute-start.10) | collective-permute-done | bytes 2912 | tf_op jit(solution)/shard_map/ppermute | solution.py:22
  77.9 2.8 collective-permute-start.12
  80.7 1.3 collective-permute-start.13
  82.2 3.0 collective-permute-done.13
  85.2 1.9 collective-permute-start.14
  87.1 3.5 collective-permute-start.15
  90.7 2.5 collective-permute-done.15
  93.4 5.4 collective-permute-start.16
  99.0 5.4 collective-permute-done.16
  105.3 4.7 copy.16
  110.1 4.1 gather_fusion
  115.8 433.0 %all-reduce.2.cloned.1.call-done = f32[128,128]{0,1:T(8,128)} async-done(((f32[128,128]{0,1:T(8,128)}), f32[128,128]{0,1:T(8,128)}) %all-reduce.2.cloned.1.call-update) | async-done | bytes 65552 | tf_op jit(solution)/shard_map/psum | solution.py:67
  550.6 11.7 %cholesky.16 = f32[128,128]{1,0:T(8,128)S(1)} custom-call(f32[128,128]{1,0:T(8,128)S(1)} %fusion.57), custom_call_target="Cholesky" | custom-call | tf_op jit(solution)/shard_map/jit(cholesky)/cholesky | solution.py:68
  563.7 9.8 %custom-call.7 = f32[1,128,128]{1,2,0:T(8,128)S(1)} custom-call(f32[1,128,128]{2,1,0:T(8,128)S(1)} %get-tuple-element.70), custom_call_target="InvertDiagBlocksLowerTriangular" | custom-call | tf_op jit(solution)/shard_map/jit(_solve_triangular)/triangular_solve | solution.py:69
  (71 shorter events, 15.2 us)
Async XLA Ops:
  7.2 43.2 %copy-start = (f32[4,8,16,128]{3,2,1,0:T(8,128)S(1)}, f32[4,8,16,128]{3,2,1,0:T(8,128)}, u32[]{:S(2)}) copy-start(f32[4,8,16,128]{3,2,1,0:T(8,128)} %param.6) | copy-start | bytes 786436
  7.2 47.7 %copy-start.4 = (s32[256]{0:T(256)S(1)}, s32[256]{0:T(256)}, u32[]{:S(2)}) copy-start(s32[256]{0:T(256)} %param.8) | copy-start | bytes 3076
  7.2 541.6 %all-reduce.2.cloned.1.call-start = ((), (), s32[]{:S(2)}) async-start(), calls=%async_computation | async-start | bytes 131072 | tf_op jit(solution)/shard_map/psum | solution.py:67
  8.3 6.2 %collective-permute-start = (f32[4,8,1,128]{3,2,1,0:T(1,128)S(1)}, f32[4,8,1,128]{3,2,1,0:T(1,128)S(1)}, u32[]{:S(2)}, u32[]{:S(2)}) collective-permute-start(f32[4,8,1,128]{3,2,1,0:T(1,128)S(1)} %get-tuple-element.67), channel_id=1, source_target_pairs={{0,8},{8,16},{16,24},{1,9},{9,17},{17,25},{2,10},{10,18},{18,26},{... | collective-permute-start | bytes 49160 | tf_op jit(solution)/shard_map/ppermute | solution.py:19
  12.2 4.5 collective-permute-start.1
  17.5 13.7 %collective-permute-start.2 = (f32[4,1,18,128]{3,2,1,0:T(8,128)S(1)}, f32[4,1,18,128]{3,2,1,0:T(8,128)S(1)}, u32[]{:S(2)}, u32[]{:S(2)}) collective-permute-start(f32[4,1,18,128]{3,2,1,0:T(8,128)S(1)} %get-tuple-element.41), channel_id=1, source_target_pairs={{32,0},{64,32},{96,64},{128,96},{160,128},{192,160},{224,192},{256... | collective-permute-start | bytes 110600 | tf_op jit(solution)/shard_map/ppermute | solution.py:22
  28.6 6.0 %collective-permute-start.3 = (f32[4,1,18,128]{3,2,1,0:T(8,128)S(1)}, f32[4,1,18,128]{3,2,1,0:T(8,128)S(1)}, u32[]{:S(2)}, u32[]{:S(2)}) collective-permute-start(f32[4,1,18,128]{3,2,1,0:T(8,128)S(1)} %get-tuple-element.40), channel_id=1, source_target_pairs={{0,32},{32,64},{64,96},{96,128},{128,160},{160,192},{192,224},{224... | collective-permute-start | bytes 110600 | tf_op jit(solution)/shard_map/ppermute | solution.py:19
  35.7 41.9 %copy-start.3 = (f32[3]{0:T(128)S(1)}, f32[3]{0:T(128)}, u32[]{:S(2)}) copy-start(f32[3]{0:T(128)} %constant.80.clone) | copy-start | bytes 40
  35.9 11.5 %collective-permute-start.4 = (f32[4,10,18,1]{3,2,1,0:T(8,128)S(1)}, f32[4,10,18,1]{3,2,1,0:T(8,128)S(1)}, u32[]{:S(2)}, u32[]{:S(2)}) collective-permute-start(f32[4,10,18,1]{3,2,1,0:T(8,128)S(1)} %get-tuple-element.31), channel_id=1, source_target_pairs={{1,0},{2,1},{3,2},{4,3},{5,4},{6,5},{7,6},{0,7},{9,8},{10,9},{11,1... | collective-permute-start | bytes 8648 | tf_op jit(solution)/shard_map/ppermute | solution.py:22
  39.4 8.0 %collective-permute-start.5 = (f32[4,10,18,1]{3,2,1,0:T(8,128)S(1)}, f32[4,10,18,1]{3,2,1,0:T(8,128)S(1)}, u32[]{:S(2)}, u32[]{:S(2)}) collective-permute-start(f32[4,10,18,1]{3,2,1,0:T(8,128)S(1)} %get-tuple-element.32), channel_id=1, source_target_pairs={{0,1},{1,2},{2,3},{3,4},{4,5},{5,6},{6,7},{7,0},{8,9},{9,10},{10,1... | collective-permute-start | bytes 8648 | tf_op jit(solution)/shard_map/ppermute | solution.py:19
  42.2 39.8 %copy-start.1 = (f32[127,3,256]{2,0,1:T(8,128)S(1)}, f32[127,3,256]{2,0,1:T(8,128)}, u32[]{:S(2)}) copy-start(f32[127,3,256]{2,0,1:T(8,128)} %param.7) | copy-start | bytes 1170436
  50.4 4.5 collective-permute-start.6
  53.6 4.5 collective-permute-start.7
  58.1 5.3 collective-permute-start.8
  60.0 6.0 %collective-permute-start.9 = (f32[4,1,18,128]{3,2,1,0:T(8,128)S(1)}, f32[4,1,18,128]{3,2,1,0:T(8,128)S(1)}, u32[]{:S(2)}, u32[]{:S(2)}) collective-permute-start(f32[4,1,18,128]{3,2,1,0:T(8,128)S(1)} %get-tuple-element.37), channel_id=1, source_target_pairs={{0,32},{32,64},{64,96},{96,128},{128,160},{160,192},{192,224},{224... | collective-permute-start | bytes 110600 | tf_op jit(solution)/shard_map/ppermute | solution.py:19
  66.3 10.9 %collective-permute-start.10 = (f32[4,10,18,1]{3,2,1,0:T(8,128)S(1)}, f32[4,10,18,1]{3,2,1,0:T(8,128)S(1)}, u32[]{:S(2)}, u32[]{:S(2)}) collective-permute-start(f32[4,10,18,1]{3,2,1,0:T(8,128)S(1)} %get-tuple-element.29), channel_id=1, source_target_pairs={{1,0},{2,1},{3,2},{4,3},{5,4},{6,5},{7,6},{0,7},{9,8},{10,9},{11,1... | collective-permute-start | bytes 8648 | tf_op jit(solution)/shard_map/ppermute | solution.py:22
  70.5 6.6 %collective-permute-start.11 = (f32[4,10,18,1]{3,2,1,0:T(8,128)S(1)}, f32[4,10,18,1]{3,2,1,0:T(8,128)S(1)}, u32[]{:S(2)}, u32[]{:S(2)}) collective-permute-start(f32[4,10,18,1]{3,2,1,0:T(8,128)S(1)} %get-tuple-element.30), channel_id=1, source_target_pairs={{0,1},{1,2},{2,3},{3,4},{4,5},{5,6},{6,7},{7,0},{8,9},{9,10},{10,1... | collective-permute-start | bytes 8648 | tf_op jit(solution)/shard_map/ppermute | solution.py:19
  77.9 4.3 collective-permute-start.12
  80.7 4.5 collective-permute-start.13
  85.2 5.5 collective-permute-start.14
  87.1 6.0 %collective-permute-start.15 = (f32[4,1,18,128]{3,2,1,0:T(8,128)S(1)}, f32[4,1,18,128]{3,2,1,0:T(8,128)S(1)}, u32[]{:S(2)}, u32[]{:S(2)}) collective-permute-start(f32[4,1,18,128]{3,2,1,0:T(8,128)S(1)} %get-tuple-element.34), channel_id=1, source_target_pairs={{0,32},{32,64},{64,96},{96,128},{128,160},{160,192},{192,224},{224... | collective-permute-start | bytes 110600 | tf_op jit(solution)/shard_map/ppermute | solution.py:19
  93.4 11.0 %collective-permute-start.16 = (f32[4,10,18,1]{3,2,1,0:T(8,128)S(1)}, f32[4,10,18,1]{3,2,1,0:T(8,128)S(1)}, u32[]{:S(2)}, u32[]{:S(2)}) collective-permute-start(f32[4,10,18,1]{3,2,1,0:T(8,128)S(1)} %get-tuple-element.27), channel_id=1, source_target_pairs={{1,0},{2,1},{3,2},{4,3},{5,4},{6,5},{7,6},{0,7},{9,8},{10,9},{11,1... | collective-permute-start | bytes 8648 | tf_op jit(solution)/shard_map/ppermute | solution.py:22
  98.9 5.8 collective-permute-start.17
  105.3 470.2 %copy-start.2 = (f32[4,8,16,128]{3,2,1,0:T(8,128)}, f32[4,8,16,128]{3,2,1,0:T(8,128)S(1)}, u32[]{:S(2)}) copy-start(f32[4,8,16,128]{3,2,1,0:T(8,128)S(1)} %fusion.15) | copy-start | bytes 786436
Sparse Core Ops, SparseCore 0:
  115.5 433.2 all-reduce.1
where the time goes:
time: 583 us; the launch traced here: 582 us
  waiting for transfers between devices  467 us (80%)
  starting transfers between devices  52 us (9%)
  other arithmetic  33.4 us (6%)
  between operations  14.5 us (2%)
  local copies, waits for them, and re-layouts  12.7 us (2%)
    psum x1, waiting for transfers between devices, local(): gram = lax.psum(local_gram, ('gx', 'gy', 'gz')) / count  433 us
    ppermute x9, starting transfers between devices, padded(): lax.ppermute(lax.slice_in_dim(block, 0, width, axis=dim), axis, backward)  32.1 us
    ppermute x9, waiting for transfers between devices, padded(): lax.ppermute(lax.slice_in_dim(block, 0, width, axis=dim), axis, backward)  25.5 us
    ppermute x9, starting transfers between devices, padded(): lax.ppermute(lax.slice_in_dim(block, block.shape[dim] - width, None, axis...  19.9 us
    another operation x3, other arithmetic, local(): lower = jnp.linalg.cholesky(gram)  12.4 us
  transfers between devices with their start and end apart: 19, of which 11 were waited for; matrix products, arithmetic and copies ran while one was open for 1% of the time, Pallas kernels for 0%

commit v1 on v0

--- a/solution.py
+++ b/solution.py
@@ -50,6 +50,10 @@
 
 
 def local(flow, basis, sample):
+
+    def skins_open(axis_tag, array_in):
+        return jax.lax.all_gather(array_in, axis_tag).sum(axis=0)
+
     points = basis.shape[2]
     modes = basis.shape[0]
     count = 3.0 * points * lax.axis_size("gx") * lax.axis_size("gy") * lax.axis_size("gz")
@@ -64,7 +68,7 @@
     local_gram = jnp.dot(
         stacked, stacked.T, precision=lax.Precision.HIGHEST, preferred_element_type=jnp.float32
     )
-    gram = lax.psum(local_gram, ("gx", "gy", "gz")) / count
+    gram = skins_open(("gx", "gy", "gz"), local_gram) / count
     lower = jnp.linalg.cholesky(gram)
     basis_next = jax.scipy.linalg.solve_triangular(lower, stacked, lower=True).reshape(
         modes + 1, 3, points

time: 583 us -> 393 us (0.67)
  waiting for transfers between devices: 467 us -> 265 us
  other arithmetic: 33.4 us -> 44.8 us
    psum x1 -> x0, waiting for transfers between devices: 433 us -> none  [local(): gram = lax.psum(local_gram, ('gx', 'gy', 'gz')) / count]
    all_gather x0 -> x1, waiting for transfers between devices: none -> 231 us  [skins_open(): return jax.lax.all_gather(array_in, axis_tag).sum(axis=0)]
    reduce_sum x0 -> x1, other arithmetic: none -> 13.1 us  [skins_open(): return jax.lax.all_gather(array_in, axis_tag).sum(axis=0)]
where the time goes in v1:
time: 393 us; the launch traced here: 392 us
  waiting for transfers between devices  265 us (67%)
  starting transfers between devices  52 us (13%)
  other arithmetic  44.8 us (11%)
  between operations  14.5 us (4%)
  local copies, waits for them, and re-layouts  12.8 us (3%)
    all_gather x1, waiting for transfers between devices, skins_open(): return jax.lax.all_gather(array_in, axis_tag).sum(axis=0)  231 us
    ppermute x9, starting transfers between devices, padded(): lax.ppermute(lax.slice_in_dim(block, 0, width, axis=dim), axis, backward)  32.1 us
    ppermute x9, waiting for transfers between devices, padded(): lax.ppermute(lax.slice_in_dim(block, 0, width, axis=dim), axis, backward)  25.7 us
    ppermute x9, starting transfers between devices, padded(): lax.ppermute(lax.slice_in_dim(block, block.shape[dim] - width, None, axis...  19.9 us
    reduce_sum x1, other arithmetic, skins_open(): return jax.lax.all_gather(array_in, axis_tag).sum(axis=0)  13.1 us
    another operation x3, other arithmetic, local(): lower = jnp.linalg.cholesky(gram)  12.4 us
    another operation x1, other arithmetic, local(): jax.scipy.linalg.solve_triangular(lower, stacked, lower=True)  9.81 us
    ppermute x9, waiting for transfers between devices, padded(): lax.ppermute(lax.slice_in_dim(block, block.shape[dim] - width, None, axis...  8.75 us
  transfers between devices with their start and end apart: 19, of which 11 were waited for; matrix products, arithmetic and copies ran while one was open for 1% of the time, Pallas kernels for 0%

profile of v1, /device:TPU:1, one launch (start us, length us, event | category | flops | bytes accessed | tf_op | source)
XLA Modules:
  0.0 392.0 jit_solution(13465562421725911790)
XLA Ops:
  8.3 3.9 %collective-permute-start = (f32[4,8,1,128]{3,2,1,0:T(1,128)S(1)}, f32[4,8,1,128]{3,2,1,0:T(1,128)S(1)}, u32[]{:S(2)}, u32[]{:S(2)}) collective-permute-start(f32[4,8,1,128]{3,2,1,0:T(1,128)S(1)} %get-tuple-element.70), channel_id=1, source_target_pairs={{0,8},{8,16},{16,24},{1,9},{9,17},{17,25},{2,10},{10,18},{18,26},{... | collective-permute-start | bytes 49160 | tf_op jit(solution)/shard_map/ppermute | solution.py:19
  12.2 1.3 collective-permute-start.1
  14.4 2.2 collective-permute-done.1
  17.5 11.1 %collective-permute-start.2 = (f32[4,1,18,128]{3,2,1,0:T(8,128)S(1)}, f32[4,1,18,128]{3,2,1,0:T(8,128)S(1)}, u32[]{:S(2)}, u32[]{:S(2)}) collective-permute-start(f32[4,1,18,128]{3,2,1,0:T(8,128)S(1)} %get-tuple-element.44), channel_id=1, source_target_pairs={{32,0},{64,32},{96,64},{128,96},{160,128},{192,160},{224,192},{256... | collective-permute-start | bytes 110600 | tf_op jit(solution)/shard_map/ppermute | solution.py:22
  28.6 1.9 collective-permute-start.3
  31.2 3.4 collective-permute-done.3
  35.9 3.5 collective-permute-start.4
  40.6 1.6 subtract_multiply_fusion.5
  42.3 5.2 %collective-permute-done.4 = f32[4,10,18,1]{3,2,1,0:T(8,128)S(1)} collective-permute-done((f32[4,10,18,1]{3,2,1,0:T(8,128)S(1)}, f32[4,10,18,1]{3,2,1,0:T(8,128)S(1)}, u32[]{:S(2)}, u32[]{:S(2)}) %collective-permute-start.4) | collective-permute-done | bytes 2912 | tf_op jit(solution)/shard_map/ppermute | solution.py:22
  47.4 1.4 subtract_multiply_fusion.4
  48.9 1.4 fusion.24
  50.4 3.1 collective-permute-start.6
  54.9 3.1 collective-permute-done.7
  58.0 1.9 collective-permute-start.8
  60.0 3.4 collective-permute-start.9
  63.4 2.6 collective-permute-done.9
  66.3 4.2 %collective-permute-start.10 = (f32[4,10,18,1]{3,2,1,0:T(8,128)S(1)}, f32[4,10,18,1]{3,2,1,0:T(8,128)S(1)}, u32[]{:S(2)}, u32[]{:S(2)}) collective-permute-start(f32[4,10,18,1]{3,2,1,0:T(8,128)S(1)} %get-tuple-element.32), channel_id=1, source_target_pairs={{1,0},{2,1},{3,2},{4,3},{5,4},{6,5},{7,6},{0,7},{9,8},{10,9},{11,1... | collective-permute-start | bytes 8648 | tf_op jit(solution)/shard_map/ppermute | solution.py:22
  70.6 6.5 %collective-permute-done.10 = f32[4,10,18,1]{3,2,1,0:T(8,128)S(1)} collective-permute-done((f32[4,10,18,1]{3,2,1,0:T(8,128)S(1)}, f32[4,10,18,1]{3,2,1,0:T(8,128)S(1)}, u32[]{:S(2)}, u32[]{:S(2)}) %collective-permute-start.10) | collective-permute-done | bytes 2912 | tf_op jit(solution)/shard_map/ppermute | solution.py:22
  77.8 2.8 collective-permute-start.12
  80.6 1.3 collective-permute-start.13
  82.0 3.2 collective-permute-done.13
  85.1 1.9 collective-permute-start.14
  87.1 3.5 collective-permute-start.15
  90.7 2.5 collective-permute-done.15
  93.4 5.4 %collective-permute-start.16 = (f32[4,10,18,1]{3,2,1,0:T(8,128)S(1)}, f32[4,10,18,1]{3,2,1,0:T(8,128)S(1)}, u32[]{:S(2)}, u32[]{:S(2)}) collective-permute-start(f32[4,10,18,1]{3,2,1,0:T(8,128)S(1)} %get-tuple-element.30), channel_id=1, source_target_pairs={{1,0},{2,1},{3,2},{4,3},{5,4},{6,5},{7,6},{0,7},{9,8},{10,9},{11,1... | collective-permute-start | bytes 8648 | tf_op jit(solution)/shard_map/ppermute | solution.py:22
  99.0 5.4 %collective-permute-done.16 = f32[4,10,18,1]{3,2,1,0:T(8,128)S(1)} collective-permute-done((f32[4,10,18,1]{3,2,1,0:T(8,128)S(1)}, f32[4,10,18,1]{3,2,1,0:T(8,128)S(1)}, u32[]{:S(2)}, u32[]{:S(2)}) %collective-permute-start.16) | collective-permute-done | bytes 2912 | tf_op jit(solution)/shard_map/ppermute | solution.py:22
  105.3 4.7 %copy.22 = f32[3,8,16,128]{0,3,2,1:T(8,128)} copy(f32[3,8,16,128]{3,2,1,0:T(8,128)S(1)} %slice.406) | data formatting | bytes 393216 | tf_op jit(solution)/shard_map/slice | solution.py:65
  110.0 4.1 %gather_fusion = f32[256,3]{1,0:T(8,128)S(1)} fusion(f32[3,16384]{0,1:T(8,128)} %bitcast.49, s32[1024]{0:T(1024)S(1)} %pad_clamp_fusion), kind=kCustom, calls=%fused_computation | custom fusion | bytes 7168 | tf_op jit(solution)/shard_map/jit(_take)/gather | solution.py:66
  115.9 231.1 %all-gather.3.cloned.1.call-done = f32[65536,128]{1,0:T(8,128)} async-done(((f32[128,128]{1,0:T(8,128)}), f32[65536,128]{1,0:T(8,128)}) %all-gather.3.cloned.1.call-update) | async-done | bytes 33554448 | tf_op jit(solution)/shard_map/all_gather | solution.py:55
  347.0 13.1 %reduce_sum.9 = f32[128,128]{1,0:T(8,128)S(1)} reduce(f32[512,128,128]{2,1,0:T(8,128)} %bitcast.48, f32[]{:T(128)} %constant.78.clone.1), dimensions={0}, to_apply=%region_0.1 | reduce | flops 8372224 | bytes 33619972 | tf_op jit(solution)/shard_map/reduce_sum | solution.py:55
  360.3 11.7 %cholesky.16 = f32[128,128]{1,0:T(8,128)S(1)} custom-call(f32[128,128]{1,0:T(8,128)S(1)} %fusion.57), custom_call_target="Cholesky" | custom-call | tf_op jit(solution)/shard_map/jit(cholesky)/cholesky | solution.py:72
  373.4 9.8 %custom-call.7 = f32[1,128,128]{1,2,0:T(8,128)S(1)} custom-call(f32[1,128,128]{2,1,0:T(8,128)S(1)} %get-tuple-element.73), custom_call_target="InvertDiagBlocksLowerTriangular" | custom-call | tf_op jit(solution)/shard_map/jit(_solve_triangular)/triangular_solve | solution.py:73
  (73 shorter events, 14.9 us)
Async XLA Ops:
  7.2 43.1 %copy-start = (f32[4,8,16,128]{3,2,1,0:T(8,128)S(1)}, f32[4,8,16,128]{3,2,1,0:T(8,128)}, u32[]{:S(2)}) copy-start(f32[4,8,16,128]{3,2,1,0:T(8,128)} %param.6) | copy-start | bytes 786436
  7.2 47.6 %copy-start.4 = (s32[256]{0:T(256)S(1)}, s32[256]{0:T(256)}, u32[]{:S(2)}) copy-start(s32[256]{0:T(256)} %param.8) | copy-start | bytes 3076
  7.2 339.8 %all-gather.3.cloned.1.call-start = ((), (), s32[]{:S(2)}) async-start(), calls=%async_computation | async-start | bytes 33619968 | tf_op jit(solution)/shard_map/all_gather | solution.py:55
  8.3 6.2 %collective-permute-start = (f32[4,8,1,128]{3,2,1,0:T(1,128)S(1)}, f32[4,8,1,128]{3,2,1,0:T(1,128)S(1)}, u32[]{:S(2)}, u32[]{:S(2)}) collective-permute-start(f32[4,8,1,128]{3,2,1,0:T(1,128)S(1)} %get-tuple-element.70), channel_id=1, source_target_pairs={{0,8},{8,16},{16,24},{1,9},{9,17},{17,25},{2,10},{10,18},{18,26},{... | collective-permute-start | bytes 49160 | tf_op jit(solution)/shard_map/ppermute | solution.py:19
  12.2 4.5 %collective-permute-start.1 = (f32[4,8,1,128]{3,2,1,0:T(1,128)S(1)}, f32[4,8,1,128]{3,2,1,0:T(1,128)S(1)}, u32[]{:S(2)}, u32[]{:S(2)}) collective-permute-start(f32[4,8,1,128]{3,2,1,0:T(1,128)S(1)} %get-tuple-element.71), channel_id=1, source_target_pairs={{8,0},{16,8},{24,16},{9,1},{17,9},{25,17},{10,2},{18,10},{26,18},{... | collective-permute-start | bytes 49160 | tf_op jit(solution)/shard_map/ppermute | solution.py:22
  17.5 13.7 %collective-permute-start.2 = (f32[4,1,18,128]{3,2,1,0:T(8,128)S(1)}, f32[4,1,18,128]{3,2,1,0:T(8,128)S(1)}, u32[]{:S(2)}, u32[]{:S(2)}) collective-permute-start(f32[4,1,18,128]{3,2,1,0:T(8,128)S(1)} %get-tuple-element.44), channel_id=1, source_target_pairs={{32,0},{64,32},{96,64},{128,96},{160,128},{192,160},{224,192},{256... | collective-permute-start | bytes 110600 | tf_op jit(solution)/shard_map/ppermute | solution.py:22
  28.6 6.0 %collective-permute-start.3 = (f32[4,1,18,128]{3,2,1,0:T(8,128)S(1)}, f32[4,1,18,128]{3,2,1,0:T(8,128)S(1)}, u32[]{:S(2)}, u32[]{:S(2)}) collective-permute-start(f32[4,1,18,128]{3,2,1,0:T(8,128)S(1)} %get-tuple-element.43), channel_id=1, source_target_pairs={{0,32},{32,64},{64,96},{96,128},{128,160},{160,192},{192,224},{224... | collective-permute-start | bytes 110600 | tf_op jit(solution)/shard_map/ppermute | solution.py:19
  35.7 41.8 %copy-start.3 = (f32[3]{0:T(128)S(1)}, f32[3]{0:T(128)}, u32[]{:S(2)}) copy-start(f32[3]{0:T(128)} %constant.81.clone) | copy-start | bytes 40
  35.9 11.5 %collective-permute-start.4 = (f32[4,10,18,1]{3,2,1,0:T(8,128)S(1)}, f32[4,10,18,1]{3,2,1,0:T(8,128)S(1)}, u32[]{:S(2)}, u32[]{:S(2)}) collective-permute-start(f32[4,10,18,1]{3,2,1,0:T(8,128)S(1)} %get-tuple-element.34), channel_id=1, source_target_pairs={{1,0},{2,1},{3,2},{4,3},{5,4},{6,5},{7,6},{0,7},{9,8},{10,9},{11,1... | collective-permute-start | bytes 8648 | tf_op jit(solution)/shard_map/ppermute | solution.py:22
  39.4 8.0 %collective-permute-start.5 = (f32[4,10,18,1]{3,2,1,0:T(8,128)S(1)}, f32[4,10,18,1]{3,2,1,0:T(8,128)S(1)}, u32[]{:S(2)}, u32[]{:S(2)}) collective-permute-start(f32[4,10,18,1]{3,2,1,0:T(8,128)S(1)} %get-tuple-element.35), channel_id=1, source_target_pairs={{0,1},{1,2},{2,3},{3,4},{4,5},{5,6},{6,7},{7,0},{8,9},{9,10},{10,1... | collective-permute-start | bytes 8648 | tf_op jit(solution)/shard_map/ppermute | solution.py:19
  50.4 4.5 %collective-permute-start.6 = (f32[4,8,1,128]{3,2,1,0:T(1,128)S(1)}, f32[4,8,1,128]{3,2,1,0:T(1,128)S(1)}, u32[]{:S(2)}, u32[]{:S(2)}) collective-permute-start(f32[4,8,1,128]{3,2,1,0:T(1,128)S(1)} %get-tuple-element.61), channel_id=1, source_target_pairs={{0,8},{8,16},{16,24},{1,9},{9,17},{17,25},{2,10},{10,18},{18,26},{... | collective-permute-start | bytes 49160 | tf_op jit(solution)/shard_map/ppermute | solution.py:19
  53.5 4.5 %collective-permute-start.7 = (f32[4,8,1,128]{3,2,1,0:T(1,128)S(1)}, f32[4,8,1,128]{3,2,1,0:T(1,128)S(1)}, u32[]{:S(2)}, u32[]{:S(2)}) collective-permute-start(f32[4,8,1,128]{3,2,1,0:T(1,128)S(1)} %get-tuple-element.62), channel_id=1, source_target_pairs={{8,0},{16,8},{24,16},{9,1},{17,9},{25,17},{10,2},{18,10},{26,18},{... | collective-permute-start | bytes 49160 | tf_op jit(solution)/shard_map/ppermute | solution.py:22
  58.0 5.3 %collective-permute-start.8 = (f32[4,1,18,128]{3,2,1,0:T(8,128)S(1)}, f32[4,1,18,128]{3,2,1,0:T(8,128)S(1)}, u32[]{:S(2)}, u32[]{:S(2)}) collective-permute-start(f32[4,1,18,128]{3,2,1,0:T(8,128)S(1)} %get-tuple-element.41), channel_id=1, source_target_pairs={{32,0},{64,32},{96,64},{128,96},{160,128},{192,160},{224,192},{256... | collective-permute-start | bytes 110600 | tf_op jit(solution)/shard_map/ppermute | solution.py:22
  60.0 6.0 %collective-permute-start.9 = (f32[4,1,18,128]{3,2,1,0:T(8,128)S(1)}, f32[4,1,18,128]{3,2,1,0:T(8,128)S(1)}, u32[]{:S(2)}, u32[]{:S(2)}) collective-permute-start(f32[4,1,18,128]{3,2,1,0:T(8,128)S(1)} %get-tuple-element.40), channel_id=1, source_target_pairs={{0,32},{32,64},{64,96},{96,128},{128,160},{160,192},{192,224},{224... | collective-permute-start | bytes 110600 | tf_op jit(solution)/shard_map/ppermute | solution.py:19
  66.3 10.9 %collective-permute-start.10 = (f32[4,10,18,1]{3,2,1,0:T(8,128)S(1)}, f32[4,10,18,1]{3,2,1,0:T(8,128)S(1)}, u32[]{:S(2)}, u32[]{:S(2)}) collective-permute-start(f32[4,10,18,1]{3,2,1,0:T(8,128)S(1)} %get-tuple-element.32), channel_id=1, source_target_pairs={{1,0},{2,1},{3,2},{4,3},{5,4},{6,5},{7,6},{0,7},{9,8},{10,9},{11,1... | collective-permute-start | bytes 8648 | tf_op jit(solution)/shard_map/ppermute | solution.py:22
  70.5 6.6 %collective-permute-start.11 = (f32[4,10,18,1]{3,2,1,0:T(8,128)S(1)}, f32[4,10,18,1]{3,2,1,0:T(8,128)S(1)}, u32[]{:S(2)}, u32[]{:S(2)}) collective-permute-start(f32[4,10,18,1]{3,2,1,0:T(8,128)S(1)} %get-tuple-element.33), channel_id=1, source_target_pairs={{0,1},{1,2},{2,3},{3,4},{4,5},{5,6},{6,7},{7,0},{8,9},{9,10},{10,1... | collective-permute-start | bytes 8648 | tf_op jit(solution)/shard_map/ppermute | solution.py:19
  77.8 4.2 %collective-permute-start.12 = (f32[4,8,1,128]{3,2,1,0:T(1,128)S(1)}, f32[4,8,1,128]{3,2,1,0:T(1,128)S(1)}, u32[]{:S(2)}, u32[]{:S(2)}) collective-permute-start(f32[4,8,1,128]{3,2,1,0:T(1,128)S(1)} %get-tuple-element.52), channel_id=1, source_target_pairs={{0,8},{8,16},{16,24},{1,9},{9,17},{17,25},{2,10},{10,18},{18,26},{... | collective-permute-start | bytes 49160 | tf_op jit(solution)/shard_map/ppermute | solution.py:19
  80.6 4.5 %collective-permute-start.13 = (f32[4,8,1,128]{3,2,1,0:T(1,128)S(1)}, f32[4,8,1,128]{3,2,1,0:T(1,128)S(1)}, u32[]{:S(2)}, u32[]{:S(2)}) collective-permute-start(f32[4,8,1,128]{3,2,1,0:T(1,128)S(1)} %get-tuple-element.53), channel_id=1, source_target_pairs={{8,0},{16,8},{24,16},{9,1},{17,9},{25,17},{10,2},{18,10},{26,18},{... | collective-permute-start | bytes 49160 | tf_op jit(solution)/shard_map/ppermute | solution.py:22
  85.1 5.5 %collective-permute-start.14 = (f32[4,1,18,128]{3,2,1,0:T(8,128)S(1)}, f32[4,1,18,128]{3,2,1,0:T(8,128)S(1)}, u32[]{:S(2)}, u32[]{:S(2)}) collective-permute-start(f32[4,1,18,128]{3,2,1,0:T(8,128)S(1)} %get-tuple-element.38), channel_id=1, source_target_pairs={{32,0},{64,32},{96,64},{128,96},{160,128},{192,160},{224,192},{256... | collective-permute-start | bytes 110600 | tf_op jit(solution)/shard_map/ppermute | solution.py:22
  87.1 6.0 %collective-permute-start.15 = (f32[4,1,18,128]{3,2,1,0:T(8,128)S(1)}, f32[4,1,18,128]{3,2,1,0:T(8,128)S(1)}, u32[]{:S(2)}, u32[]{:S(2)}) collective-permute-start(f32[4,1,18,128]{3,2,1,0:T(8,128)S(1)} %get-tuple-element.37), channel_id=1, source_target_pairs={{0,32},{32,64},{64,96},{96,128},{128,160},{160,192},{192,224},{224... | collective-permute-start | bytes 110600 | tf_op jit(solution)/shard_map/ppermute | solution.py:19
  93.4 11.0 %collective-permute-start.16 = (f32[4,10,18,1]{3,2,1,0:T(8,128)S(1)}, f32[4,10,18,1]{3,2,1,0:T(8,128)S(1)}, u32[]{:S(2)}, u32[]{:S(2)}) collective-permute-start(f32[4,10,18,1]{3,2,1,0:T(8,128)S(1)} %get-tuple-element.30), channel_id=1, source_target_pairs={{1,0},{2,1},{3,2},{4,3},{5,4},{6,5},{7,6},{0,7},{9,8},{10,9},{11,1... | collective-permute-start | bytes 8648 | tf_op jit(solution)/shard_map/ppermute | solution.py:22
  98.8 15.4 %copy-start.1 = (f32[127,3,256]{2,0,1:T(8,128)S(1)}, f32[127,3,256]{2,0,1:T(8,128)}, u32[]{:S(2)}) copy-start(f32[127,3,256]{2,0,1:T(8,128)} %param.7) | copy-start | bytes 1170436
  98.8 5.8 %collective-permute-start.17 = (f32[4,10,18,1]{3,2,1,0:T(8,128)S(1)}, f32[4,10,18,1]{3,2,1,0:T(8,128)S(1)}, u32[]{:S(2)}, u32[]{:S(2)}) collective-permute-start(f32[4,10,18,1]{3,2,1,0:T(8,128)S(1)} %get-tuple-element.31), channel_id=1, source_target_pairs={{0,1},{1,2},{2,3},{3,4},{4,5},{5,6},{6,7},{7,0},{8,9},{9,10},{10,1... | collective-permute-start | bytes 8648 | tf_op jit(solution)/shard_map/ppermute | solution.py:19
  105.2 254.8 %copy-start.2 = (f32[4,8,16,128]{3,2,1,0:T(8,128)}, f32[4,8,16,128]{3,2,1,0:T(8,128)S(1)}, u32[]{:S(2)}) copy-start(f32[4,8,16,128]{3,2,1,0:T(8,128)S(1)} %fusion.15) | copy-start | bytes 786436
Sparse Core Ops, SparseCore 0:
  115.5 231.4 all-gather.2
